TPU v7x, 128 devices: a whole 4x4x4 slice. The times are simulated.
128 devices in a mesh: seq: 16 (over z, x), hid: 4 (over y), rep: 2 (over core).
Axes of the slice: x: 4, y: 4, z: 4, core: 2. Of those that a mesh axis runs over, the one named last changes fastest.
Arguments:
- tokens: bfloat16 [16384, 5376], P(('rep', 'seq'), 'hid'), parts along dimension 0, may hold values from -6 to 6
- norm_gain: float32 [5376], replicated, may hold values from 0.1 to 1.9
- w_query: bfloat16 [5376, 4096], P('seq', 'hid'), may hold values from -0.078125 to 0.078125
- w_key: bfloat16 [5376, 2048], P('seq', 'hid'), may hold values from -0.078125 to 0.078125
- w_value: bfloat16 [5376, 2048], P('seq', 'hid'), may hold values from -0.078125 to 0.078125
- query_gain: float32 [128], replicated, may hold values from 0.5 to 8
- key_gain: float32 [128], replicated, may hold values from 0.5 to 8
- w_out: bfloat16 [4096, 5376], P('hid', 'seq'), may hold values from -0.09375 to 0.09375
Outputs:
- attended: bfloat16 [16384, 5376], P(('rep', 'seq'), 'hid'), parts along dimension 0
There are 2 independent parts, one for each index of `rep`. A program takes and returns all parts, laid end to end along the dimension named above; an argument that names none is the same for every part. Nothing has to cross between parts.
All inputs are finite; a program needn't handle non-finite values.
Results may differ from a plain program's by a relative error of at most 0.023.
The roundings to bfloat16 on the way count: a program that leaves them out, or rounds other values in their place, can miss the bound.
Values may be sent and summed in bfloat16 or wider, within the bound.
A program may use at most 128 MiB of HBM per device.

v0:
```python
import jax
import jax.numpy as jnp
from jax import lax
from jax.sharding import PartitionSpec as P

HEAD_WIDTH = 128
WINDOW = 1024
QSCALE = 168
DEPTH = 2


def shifted(x, axis, by):
    count = lax.axis_size(axis)
    pairs = [(i, i + by) for i in range(count) if 0 <= i + by < count]
    return lax.ppermute(x, axis, pairs)


def rope(heads, positions):
    half = heads.shape[-1] // 2
    freq = 10000.0 ** (-(jnp.arange(half, dtype=jnp.float32) * 2.0) / heads.shape[-1])
    angle = positions[:, None] * freq[None, :]
    cosine = jnp.cos(angle)[:, None, :]
    sine = jnp.sin(angle)[:, None, :]
    first = heads[..., :half]
    second = heads[..., half:]
    return jnp.concatenate(
        [first * cosine - second * sine, second * cosine + first * sine], axis=-1
    )


def head_norm(heads, gain):
    return heads * lax.rsqrt(jnp.mean(heads * heads, axis=-1, keepdims=True) + 1e-06) * gain


def add_rows(normed, piece):
    return jnp.dot(normed, piece, preferred_element_type=jnp.float32)


def shards(tokens, norm_gain, w_query, w_key, w_value, query_gain, key_gain, w_out):
    whole = lax.all_gather(tokens, "hid", axis=1, tiled=True)
    xfloat = whole.astype(jnp.float32)
    normed = (
        xfloat * lax.rsqrt(jnp.mean(xfloat * xfloat, axis=-1, keepdims=True) + 1e-06) * norm_gain
    ).astype(jnp.bfloat16)
    rows = normed.shape[0]

    def add_one(piece):
        return add_rows(normed, piece)

    query = add_one(lax.all_gather(w_query, "seq", axis=0, tiled=True))
    key = add_one(lax.all_gather(w_key, "seq", axis=0, tiled=True))
    value = add_one(lax.all_gather(w_value, "seq", axis=0, tiled=True))
    local_heads = w_query.shape[1] // HEAD_WIDTH
    local_kv = w_key.shape[1] // HEAD_WIDTH
    base = lax.axis_index("seq") * rows
    qpos = base + jnp.arange(rows, dtype=jnp.int32)
    positions = qpos.astype(jnp.float32)
    qh = (
        rope(head_norm(query.reshape(rows, local_heads, HEAD_WIDTH), query_gain), positions)
        * QSCALE ** (-0.5)
    ).astype(jnp.bfloat16)
    kh = rope(head_norm(key.reshape(rows, local_kv, HEAD_WIDTH), key_gain), positions).astype(
        jnp.bfloat16
    )
    value_head = value.reshape(rows, local_kv, HEAD_WIDTH).astype(jnp.bfloat16)
    key_blocks = []
    value_blocks = []
    for distance in range(1, DEPTH + 1):
        arrived = shifted((kh, value_head), "seq", distance)
        key_blocks.insert(0, arrived[0])
        value_blocks.insert(0, arrived[1])
    keys = jnp.concatenate(key_blocks + [kh], axis=0)
    values = jnp.concatenate(value_blocks + [value_head], axis=0)
    window_extent = keys.shape[0]
    kpos = base - DEPTH * rows + jnp.arange(window_extent, dtype=jnp.int32)
    diff = qpos[:, None] - kpos[None, :]
    allowed = (diff >= 0) & (diff < WINDOW) & (kpos >= 0)[None, :]
    group = local_heads // local_kv
    grouped = qh.reshape(rows, local_kv, group, HEAD_WIDTH).transpose(1, 0, 2, 3)

    def one_head(operands):
        qpart, kpart, vpart = operands
        scores = jnp.einsum("rgd,ld->grl", qpart, kpart, preferred_element_type=jnp.float32)
        scores = jnp.where(allowed[None], scores, -jnp.inf)
        probs = jax.nn.softmax(scores, axis=-1).astype(jnp.bfloat16)
        mixed = jnp.einsum("grl,ld->rgd", probs, vpart, preferred_element_type=jnp.float32)
        return mixed.astype(jnp.bfloat16)

    per_head = lax.map(one_head, (grouped, keys.transpose(1, 0, 2), values.transpose(1, 0, 2)))
    heads_out = per_head.transpose(1, 0, 2, 3).reshape(rows, local_heads * HEAD_WIDTH)
    terms = jnp.dot(
        heads_out,
        lax.all_gather(w_out, "seq", axis=1, tiled=True),
        preferred_element_type=jnp.float32,
    )
    return lax.psum_scatter(terms.astype(jnp.bfloat16), "hid", scatter_dimension=1, tiled=True)


def solution(mesh):
    return jax.shard_map(
        shards,
        mesh=mesh,
        in_specs=(
            P(("rep", "seq"), "hid"),
            P(),
            P("seq", "hid"),
            P("seq", "hid"),
            P("seq", "hid"),
            P(),
            P(),
            P("hid", "seq"),
        ),
        out_specs=P(("rep", "seq"), "hid"),
        check_vma=False,
    )
```

profile of v0, /device:TPU:1, one launch (start us, length us, event | category | flops | bytes accessed | tf_op | source)
XLA Modules:
  0.0 466.9 jit_solution(10605443407271170900)
XLA Ops:
  6.5 0.0 all-gather.6.cloned.1.call-start
  6.5 0.7 all-gather.6.cloned.1.call-update
  7.3 0.0 all-gather.10.cloned.1.call-start
  7.3 0.7 all-gather.10.cloned.1.call-update
  8.0 0.0 all-gather.8.cloned.1.call-start
  8.1 0.7 all-gather.8.cloned.1.call-update
  8.7 0.0 all-gather.12.cloned.1.call-start
  8.8 0.5 all-gather.12.cloned.1.call-update
  9.3 0.0 all-gather.14.cloned.1.call-start
  9.4 0.5 all-gather.14.cloned.1.call-update
  9.9 0.0 reduce-scatter.2.cloned.1.call-start
  10.0 1.0 multiply_cosine_fusion
  11.0 60.4 %all-gather.6.cloned.1.call-done = bf16[512,5376]{0,1:T(8,128)(2,1)} async-done(((bf16[512,1344]{0,1:T(8,128)(2,1)}), bf16[512,5376]{0,1:T(8,128)(2,1)}) %all-gather.6.cloned.1.call-update) | async-done | bytes 5505040 | tf_op jit(solution)/shard_map/all_gather | solution.py:40
  71.4 3.8 fusion.41
  75.2 56.7 %all-gather.10.cloned.1.call-done = bf16[5376,512]{1,0:T(8,128)(2,1)} async-done(((bf16[336,512]{1,0:T(8,128)(2,1)}), bf16[5376,512]{1,0:T(8,128)(2,1)}) %all-gather.10.cloned.1.call-update) | async-done | bytes 5505040 | tf_op jit(solution)/shard_map/all_gather | solution.py:51
  131.9 7.6 %multiply_reduce_fusion.1 = (f32[512,4]{0,1:T(4,128)S(1)}, f32[512,512]{0,1:T(8,128)S(1)}) fusion(bf16[5376,512]{1,0:T(8,128)(2,1)} %all-gather.10.cloned.1.call-done, bf16[512,5376]{0,1:T(8,128)(2,1)} %all-gather.6.cloned.1.call-done, f32[5376]{0:T(1024)S(1)} %copy-done.2, f32[512]{0:T(512)S(1)} %add_rsqrt_fusion.2), kind=kOutput, calls=%fused_computation.52 | convolution fusion | flops 2830104576 | bytes 12090368 | tf_op jit(solution)/shard_map/dot_general | solution.py:36
  139.5 0.3 copy.19
  139.9 0.0 copy-done
  139.9 0.3 multiply_multiply_fusion.1
  140.2 0.5 subtract_convert_fusion
  140.7 0.3 pad_maximum_fusion
  141.0 4.6 collective-permute-start.2
  145.6 2.2 collective-permute-start.3
  147.9 54.8 %all-gather.8.cloned.1.call-done = bf16[5376,512]{1,0:T(8,128)(2,1)} async-done(((bf16[336,512]{1,0:T(8,128)(2,1)}), bf16[5376,512]{1,0:T(8,128)(2,1)}) %all-gather.8.cloned.1.call-update) | async-done | bytes 5505040 | tf_op jit(solution)/shard_map/all_gather | solution.py:52
  202.7 8.4 %convolution_convert_fusion.1 = bf16[512,512]{0,1:T(8,128)(2,1)} fusion(bf16[5376,512]{1,0:T(8,128)(2,1)} %all-gather.8.cloned.1.call-done, bf16[512,5376]{0,1:T(8,128)(2,1)} %all-gather.6.cloned.1.call-done, f32[5376]{0:T(1024)S(1)} %copy-done.2, f32[512]{0:T(512)S(1)} %add_rsqrt_fusion.2), kind=kOutput, calls=%fused_computation.47 | convolution fusion | flops 2829844480 | bytes 11557888 | tf_op jit(solution)/shard_map/dot_general | solution.py:36
  211.1 5.4 %collective-permute-start = (bf16[512,4,128]{0,2,1:T(8,128)(2,1)}, bf16[512,4,128]{0,2,1:T(8,128)(2,1)}, u32[]{:S(2)}, u32[]{:S(2)}) collective-permute-start(bf16[512,4,128]{0,2,1:T(8,128)(2,1)} %bitcast), channel_id=1, source_target_pairs={{0,16},{8,24},{16,32},{24,40},{32,48},{40,56},{48,64},{56,72},{64,... | collective-permute-start | bytes 1572872 | tf_op jit(solution)/shard_map/ppermute | solution.py:15
  216.5 3.0 collective-permute-start.1
  219.5 0.0 collective-permute-done.2
  219.5 0.0 collective-permute-done.3
  219.6 1.5 maximum_bitcast_fusion.1
  221.1 12.3 %collective-permute-done = bf16[512,4,128]{0,2,1:T(8,128)(2,1)} collective-permute-done((bf16[512,4,128]{0,2,1:T(8,128)(2,1)}, bf16[512,4,128]{0,2,1:T(8,128)(2,1)}, u32[]{:S(2)}, u32[]{:S(2)}) %collective-permute-start) | collective-permute-done | bytes 524320 | tf_op jit(solution)/shard_map/ppermute | solution.py:15
  233.4 15.0 %collective-permute-done.1 = bf16[512,4,128]{0,2,1:T(8,128)(2,1)} collective-permute-done((bf16[512,4,128]{0,2,1:T(8,128)(2,1)}, bf16[512,4,128]{0,2,1:T(8,128)(2,1)}, u32[]{:S(2)}, u32[]{:S(2)}) %collective-permute-start.1) | collective-permute-done | bytes 524320 | tf_op jit(solution)/shard_map/ppermute | solution.py:15
  248.5 2.6 maximum_bitcast_fusion
  251.0 55.3 %all-gather.12.cloned.1.call-done = bf16[5376,1024]{1,0:T(8,128)(2,1)} async-done(((bf16[336,1024]{1,0:T(8,128)(2,1)}), bf16[5376,1024]{1,0:T(8,128)(2,1)}) %all-gather.12.cloned.1.call-update) | async-done | bytes 11010064 | tf_op jit(solution)/shard_map/all_gather | solution.py:50
  306.4 11.7 %convolution_bitcast_fusion = f32[64,8,8,128]{3,1,2,0:T(8,128)S(1)} fusion(bf16[5376,1024]{1,0:T(8,128)(2,1)} %all-gather.12.cloned.1.call-done, bf16[512,5376]{0,1:T(8,128)(2,1)} %all-gather.6.cloned.1.call-done, f32[5376]{0:T(1024)S(1)} %copy-done.2, f32[512]{0:T(512)S(1)} %add_rsqrt_fusion.2), kind=kOutput, calls=%fused_computation.44 | convolution fusion | flops 5648154624 | bytes 18635776 | tf_op jit(solution)/shard_map/dot_general | solution.py:36
  318.1 0.0 copy-start.1
  318.1 0.5 copy.25
  318.6 0.6 multiply_reduce_fusion
  319.2 0.1 copy.20
  319.3 0.1 copy.21
  319.4 0.9 multiply_multiply_fusion
  320.3 1.2 multiply_subtract_fusion
  321.5 0.4 copy.22
  321.9 0.4 copy.23
  322.3 0.0 copy-start.3
  322.4 0.6 fusion.45
  323.0 0.6 copy-done.3
  323.6 43.2 %while.11 = (s32[]{:T(128)}, bf16[4,512,2,128]{1,3,2,0:T(8,128)(2,1)S(1)}, bf16[4,1536,128]{1,2,0:T(8,128)(2,1)}, bf16[4,1536,128]{2,1,0:T(8,128)(2,1)}, bf16[4,...) while((s32[]{:T(128)}, ...), condition=%wide.region_6.7_spmd.clone, body=%wide.region_3.6_spmd.clone.sunk | while | flops 817235456 | bytes 15486557 | solution.py:89
  323.6 1.2 fusion.74
  324.8 5.8 %fusion.75 = (f32[2,512]{1,0:T(2,128)S(1)}, f32[2,512,1536]{1,2,0:T(8,128)}) fusion(pred[512,1536]{0,1:T(8,128)(4,1)S(1)} %fusion.74, bf16[4,1536,128]{2,1,0:T(8,128)(2,1)} %get-tuple-element.159, s32[]{:T(128)} %get-tuple-element.147, bf16[4,512,2,128]{3,1,2,0:T(8,128)(2,1)S(1)} %get-tuple-element.160), kind=kOutput, calls=%fused_computation.65.clone.1 | convolution fusion | flops 407373312 | bytes 7738368 | tf_op jit(solution)/shard_map/while/body/eval_jaxpr/sub | solution.py:85
  330.6 3.6 fusion.76
  334.2 1.2 fusion.74
  335.4 5.8 %fusion.75 = (f32[2,512]{1,0:T(2,128)S(1)}, f32[2,512,1536]{1,2,0:T(8,128)}) fusion(pred[512,1536]{0,1:T(8,128)(4,1)S(1)} %fusion.74, bf16[4,1536,128]{2,1,0:T(8,128)(2,1)} %get-tuple-element.159, s32[]{:T(128)} %get-tuple-element.147, bf16[4,512,2,128]{3,1,2,0:T(8,128)(2,1)S(1)} %get-tuple-element.160), kind=kOutput, calls=%fused_computation.65.clone.1 | convolution fusion | flops 407373312 | bytes 7738368 | tf_op jit(solution)/shard_map/while/body/eval_jaxpr/sub | solution.py:85
  341.2 4.3 fusion.76
  345.6 1.2 fusion.74
  346.8 5.8 %fusion.75 = (f32[2,512]{1,0:T(2,128)S(1)}, f32[2,512,1536]{1,2,0:T(8,128)}) fusion(pred[512,1536]{0,1:T(8,128)(4,1)S(1)} %fusion.74, bf16[4,1536,128]{2,1,0:T(8,128)(2,1)} %get-tuple-element.159, s32[]{:T(128)} %get-tuple-element.147, bf16[4,512,2,128]{3,1,2,0:T(8,128)(2,1)S(1)} %get-tuple-element.160), kind=kOutput, calls=%fused_computation.65.clone.1 | convolution fusion | flops 407373312 | bytes 7738368 | tf_op jit(solution)/shard_map/while/body/eval_jaxpr/sub | solution.py:85
  352.6 3.6 fusion.76
  356.2 1.2 fusion.74
  357.4 5.8 %fusion.75 = (f32[2,512]{1,0:T(2,128)S(1)}, f32[2,512,1536]{1,2,0:T(8,128)}) fusion(pred[512,1536]{0,1:T(8,128)(4,1)S(1)} %fusion.74, bf16[4,1536,128]{2,1,0:T(8,128)(2,1)} %get-tuple-element.159, s32[]{:T(128)} %get-tuple-element.147, bf16[4,512,2,128]{3,1,2,0:T(8,128)(2,1)S(1)} %get-tuple-element.160), kind=kOutput, calls=%fused_computation.65.clone.1 | convolution fusion | flops 407373312 | bytes 7738368 | tf_op jit(solution)/shard_map/while/body/eval_jaxpr/sub | solution.py:85
  363.2 3.5 fusion.76
  366.8 24.1 %all-gather.14.cloned.1.call-done = bf16[1024,5376]{0,1:T(8,128)(2,1)} async-done(((bf16[1024,336]{0,1:T(8,128)(2,1)}), bf16[1024,5376]{0,1:T(8,128)(2,1)}) %all-gather.14.cloned.1.call-update) | async-done | bytes 11010064 | tf_op jit(solution)/shard_map/all_gather | solution.py:93
  390.9 11.8 %convolution_convert_fusion = bf16[512,5376]{0,1:T(8,128)(2,1)} fusion(bf16[1024,5376]{0,1:T(8,128)(2,1)} %all-gather.14.cloned.1.call-done, bf16[512,1024]{0,1:T(8,128)(2,1)S(1)} %bitcast.83), kind=kOutput, calls=%fused_computation.37 | convolution fusion | flops 5639897088 | bytes 17563648 | tf_op jit(solution)/shard_map/dot_general | solution.py:91
  402.7 0.0 reduce-scatter.2.cloned.1.call-update
  402.7 57.3 %reduce-scatter.2.cloned.1.call-done = bf16[512,1344]{0,1:T(8,128)(2,1)} async-done(((bf16[512,5376]{0,1:T(8,128)(2,1)}), bf16[512,1344]{0,1:T(8,128)(2,1)}) %reduce-scatter.2.cloned.1.call-update) | async-done | bytes 1376272 | tf_op jit(solution)/shard_map/reduce_scatter | solution.py:96
  (13 shorter events, 0.1 us)
Async XLA Ops:
  6.5 64.9 %all-gather.6.cloned.1.call-start = ((), (), s32[]{:S(2)}) async-start(), calls=%async_computation.1 | async-start | bytes 6881280 | tf_op jit(solution)/shard_map/all_gather | solution.py:40
  7.3 124.7 %all-gather.10.cloned.1.call-start = ((), (), s32[]{:S(2)}) async-start(), calls=%async_computation.3 | async-start | bytes 5849088 | tf_op jit(solution)/shard_map/all_gather | solution.py:51
  8.0 194.7 %all-gather.8.cloned.1.call-start = ((), (), s32[]{:S(2)}) async-start(), calls=%async_computation.2 | async-start | bytes 5849088 | tf_op jit(solution)/shard_map/all_gather | solution.py:52
  8.7 297.6 %all-gather.12.cloned.1.call-start = ((), (), s32[]{:S(2)}) async-start(), calls=%async_computation.4 | async-start | bytes 11698176 | tf_op jit(solution)/shard_map/all_gather | solution.py:50
  9.3 381.6 %all-gather.14.cloned.1.call-start = ((), (), s32[]{:S(2)}) async-start(), calls=%async_computation.5 | async-start | bytes 11698176 | tf_op jit(solution)/shard_map/all_gather | solution.py:93
  9.9 122.0 %copy-start.2 = (f32[5376]{0:T(1024)S(1)}, f32[5376]{0:T(1024)}, u32[]{:S(2)}) copy-start(f32[5376]{0:T(1024)} %param.11) | copy-start | bytes 64516
  9.9 450.1 %reduce-scatter.2.cloned.1.call-start = ((), (), s32[]{:S(2)}) async-start(), calls=%async_computation.6 | async-start | bytes 6881280 | tf_op jit(solution)/shard_map/reduce_scatter | solution.py:96
  75.2 64.7 %copy-start = (f32[128]{0:T(128)S(1)}, f32[128]{0:T(128)}, u32[]{:S(2)}) copy-start(f32[128]{0:T(128)} %param.16) | copy-start | bytes 1540
  141.0 78.6 %collective-permute-start.2 = (bf16[512,4,128]{2,0,1:T(8,128)(2,1)S(1)}, bf16[512,4,128]{2,0,1:T(8,128)(2,1)S(1)}, u32[]{:S(2)}, u32[]{:S(2)}) collective-permute-start(bf16[512,4,128]{2,0,1:T(8,128)(2,1)S(1)} %pad_maximum_fusion), channel_id=1, source_target_pairs={{0,16},{8,24},{16,32},{24,40},{32,48},{40,56},{48,64},{56,72},{64,... | collective-permute-start | bytes 1572872 | tf_op jit(solution)/shard_map/ppermute | solution.py:15
  145.6 73.9 %collective-permute-start.3 = (bf16[512,4,128]{2,0,1:T(8,128)(2,1)S(1)}, bf16[512,4,128]{2,0,1:T(8,128)(2,1)S(1)}, u32[]{:S(2)}, u32[]{:S(2)}) collective-permute-start(bf16[512,4,128]{2,0,1:T(8,128)(2,1)S(1)} %pad_maximum_fusion), channel_id=1, source_target_pairs={{0,8},{8,16},{16,24},{24,32},{32,40},{40,48},{48,56},{56,64},{64,7... | collective-permute-start | bytes 1572872 | tf_op jit(solution)/shard_map/ppermute | solution.py:15
  211.1 22.3 %collective-permute-start = (bf16[512,4,128]{0,2,1:T(8,128)(2,1)}, bf16[512,4,128]{0,2,1:T(8,128)(2,1)}, u32[]{:S(2)}, u32[]{:S(2)}) collective-permute-start(bf16[512,4,128]{0,2,1:T(8,128)(2,1)} %bitcast), channel_id=1, source_target_pairs={{0,16},{8,24},{16,32},{24,40},{32,48},{40,56},{48,64},{56,72},{64,... | collective-permute-start | bytes 1572872 | tf_op jit(solution)/shard_map/ppermute | solution.py:15
  216.5 31.9 %collective-permute-start.1 = (bf16[512,4,128]{0,2,1:T(8,128)(2,1)}, bf16[512,4,128]{0,2,1:T(8,128)(2,1)}, u32[]{:S(2)}, u32[]{:S(2)}) collective-permute-start(bf16[512,4,128]{0,2,1:T(8,128)(2,1)} %bitcast), channel_id=1, source_target_pairs={{0,8},{8,16},{16,24},{24,32},{32,40},{40,48},{48,56},{56,64},{64,7... | collective-permute-start | bytes 1572872 | tf_op jit(solution)/shard_map/ppermute | solution.py:15
  318.1 1.4 copy-start.1
  322.3 1.2 copy-start.3
Sparse Core Ops, SparseCore 0:
  9.0 62.3 all-gather.5
  73.5 58.3 all-gather.9
  134.1 68.5 all-gather.7
  204.7 101.6 all-gather.11
  308.3 82.4 all-gather.13
  402.8 57.1 reduce-scatter.1
where the time goes:
time: 467 us
  waiting for transfers between devices  339 us (73%)
  matrix products  77.8 us (17%)
  other arithmetic  18.1 us (4%)
  starting transfers between devices  15.5 us (3%)
  between operations  13.7 us (3%)
    all_gather x1, waiting for transfers between devices, shards(): whole = lax.all_gather(tokens, 'hid', axis=1, tiled=True)  60.4 us
    reduce_scatter x1, waiting for transfers between devices, shards(): lax.psum_scatter(terms.astype(jnp.bfloat16), 'hid', scatter_dimension=1,...  57.3 us
    all_gather x1, waiting for transfers between devices, shards(): key = add_one(lax.all_gather(w_key, 'seq', axis=0, tiled=True))  56.7 us
    all_gather x1, waiting for transfers between devices, shards(): query = add_one(lax.all_gather(w_query, 'seq', axis=0, tiled=True))  55.3 us
    all_gather x1, waiting for transfers between devices, shards(): value = add_one(lax.all_gather(w_value, 'seq', axis=0, tiled=True))  54.8 us
    dot_general x3, matrix products, add_rows(): return jnp.dot(normed, piece, preferred_element_type=jnp.float32)  27.7 us
    ppermute x4, waiting for transfers between devices, shifted(): return lax.ppermute(x, axis, pairs)  27.4 us
    all_gather x1, waiting for transfers between devices, shards(): lax.all_gather(w_out, 'seq', axis=1, tiled=True)  24.1 us
  transfers between devices with their start and end apart: 10, of which 8 were waited for; matrix products, arithmetic and copies ran while one was open for 18% of the time, Pallas kernels for 0%

commit v1 on v0

--- a/solution.py
+++ b/solution.py
@@ -37,7 +37,12 @@
 
 
 def shards(tokens, norm_gain, w_query, w_key, w_value, query_gain, key_gain, w_out):
-    whole = lax.all_gather(tokens, "hid", axis=1, tiled=True)
+    ring = [tokens]
+    for hop in range(3):
+        ring.append(lax.ppermute(ring[-1], "hid", [(dev, (dev + 1) % 4) for dev in range(4)]))
+    whole = jnp.roll(
+        jnp.concatenate(ring[::-1], axis=1), (lax.axis_index("hid") + 1) * ring[0].shape[1], axis=1
+    )
     xfloat = whole.astype(jnp.float32)
     normed = (
         xfloat * lax.rsqrt(jnp.mean(xfloat * xfloat, axis=-1, keepdims=True) + 1e-06) * norm_gain

time: 467 us -> 394 us (0.84)
  waiting for transfers between devices: 339 us -> 252 us
  local copies, waits for them, and re-layouts: 2.44 us -> 12 us
    ppermute x0 -> x3, waiting for transfers between devices: none -> 92.9 us  [shards(): lax.ppermute(ring[-1], 'hid', [(dev, (dev + 1) % 4) for dev in range(4)])]
    all_gather x1 -> x0, waiting for transfers between devices: 60.4 us -> none  [shards(): whole = lax.all_gather(tokens, 'hid', axis=1, tiled=True)]
    all_gather x1, waiting for transfers between devices: 56.7 us -> 0.02 us  [shards(): key = add_one(lax.all_gather(w_key, 'seq', axis=0, tiled=True))]
    all_gather x1, waiting for transfers between devices: 54.8 us -> 0.02 us  [shards(): value = add_one(lax.all_gather(w_value, 'seq', axis=0, tiled=True))]
    unnamed x9 -> x18, local copies, waits for them, and re-layouts: 1.08 us -> 10.5 us
    all_gather x1, waiting for transfers between devices: 55.3 us -> 48 us  [shards(): query = add_one(lax.all_gather(w_query, 'seq', axis=0, tiled=True))]
  transfers between devices with their start and end apart: 10 -> 12, of which waited for: 8 -> 9; matrix products, arithmetic and copies ran while one was open for 18% -> 24% of each run, Pallas kernels for 0% -> 0%
where the time goes in v1:
time: 394 us
  waiting for transfers between devices  252 us (64%)
  matrix products  81.5 us (21%)
  starting transfers between devices  18.9 us (5%)
  other arithmetic  16.3 us (4%)
  between operations  13.4 us (3%)
  local copies, waits for them, and re-layouts  12 us (3%)
    ppermute x3, waiting for transfers between devices, shards(): lax.ppermute(ring[-1], 'hid', [(dev, (dev + 1) % 4) for dev in range(4)])  92.9 us
    reduce_scatter x1, waiting for transfers between devices, shards(): lax.psum_scatter(terms.astype(jnp.bfloat16), 'hid', scatter_dimension=1,...  57.3 us
    all_gather x1, waiting for transfers between devices, shards(): query = add_one(lax.all_gather(w_query, 'seq', axis=0, tiled=True))  48 us
    ppermute x4, waiting for transfers between devices, shifted(): return lax.ppermute(x, axis, pairs)  29.9 us
    dot_general x3, matrix products, add_rows(): return jnp.dot(normed, piece, preferred_element_type=jnp.float32)  29.6 us
    sub x4, matrix products, one_head(): probs = jax.nn.softmax(scores, axis=-1).astype(jnp.bfloat16)  23.3 us
    all_gather x1, waiting for transfers between devices, shards(): lax.all_gather(w_out, 'seq', axis=1, tiled=True)  20.8 us
    dot_general x4, matrix products, one_head(): jnp.einsum('grl,ld->rgd', probs, vpart, preferred_element_type=jnp.float32)  18.2 us
  transfers between devices with their start and end apart: 12, of which 9 were waited for; matrix products, arithmetic and copies ran while one was open for 24% of the time, Pallas kernels for 0%

profile of v1, /device:TPU:1, one launch (start us, length us, event | category | flops | bytes accessed | tf_op | source)
XLA Modules:
  0.0 393.8 jit_solution(3031363065526724523)
XLA Ops:
  6.5 0.7 all-gather.7.cloned.1.call-update
  7.3 0.0 all-gather.5.cloned.1.call-start
  7.3 0.7 all-gather.5.cloned.1.call-update
  8.0 0.0 all-gather.9.cloned.1.call-start
  8.1 0.7 all-gather.9.cloned.1.call-update
  8.7 0.0 all-gather.11.cloned.1.call-start
  8.8 0.5 all-gather.11.cloned.1.call-update
  9.4 2.2 collective-permute-start
  11.6 31.4 %collective-permute-done = bf16[512,1344]{0,1:T(8,128)(2,1)S(1)} collective-permute-done((bf16[512,1344]{0,1:T(8,128)(2,1)}, bf16[512,1344]{0,1:T(8,128)(2,1)S(1)}, u32[]{:S(2)}, u32[]{:S(2)}) %collective-permute-start) | collective-permute-done | bytes 1376288 | tf_op jit(solution)/shard_map/ppermute | solution.py:42
  43.0 31.6 %collective-permute-done.1 = bf16[512,1344]{0,1:T(8,128)(2,1)} collective-permute-done((bf16[512,1344]{0,1:T(8,128)(2,1)S(1)}, bf16[512,1344]{0,1:T(8,128)(2,1)}, u32[]{:S(2)}, u32[]{:S(2)}) %collective-permute-start.1) | collective-permute-done | bytes 1376288 | tf_op jit(solution)/shard_map/ppermute | solution.py:42
  74.6 1.0 multiply_cosine_fusion
  75.6 29.9 %collective-permute-done.2 = bf16[512,1344]{0,1:T(8,128)(2,1)} collective-permute-done((bf16[512,1344]{0,1:T(8,128)(2,1)}, bf16[512,1344]{0,1:T(8,128)(2,1)}, u32[]{:S(2)}, u32[]{:S(2)}) %collective-permute-start.2) | collective-permute-done | bytes 1376288 | tf_op jit(solution)/shard_map/ppermute | solution.py:42
  105.5 1.4 constant_dynamic-update-slice_fusion.7
  106.9 1.4 constant_dynamic-update-slice_fusion.6
  108.3 0.1 constant_dynamic-update-slice_fusion.5
  108.4 0.1 constant_dynamic-update-slice_fusion.4
  108.5 1.4 constant_dynamic-update-slice_fusion.3
  110.0 1.5 constant_dynamic-update-slice_fusion.2
  111.5 0.1 constant_dynamic-update-slice_fusion.1
  111.6 0.1 constant_dynamic-update-slice_fusion
  111.7 4.0 %copy-done.1 = bf16[512,10752]{0,1:T(8,128)(2,1)} copy-done((bf16[512,10752]{0,1:T(8,128)(2,1)}, bf16[512,10752]{0,1:T(8,128)(2,1)S(1)}, u32[]{:S(2)}) %copy-start.1) | copy-done | bytes 11010072
  115.7 1.9 fusion.41
  117.6 8.6 %multiply_reduce_fusion.1 = (f32[512,4]{0,1:T(4,128)S(1)}, f32[512,512]{0,1:T(8,128)S(1)}) fusion(bf16[5376,512]{1,0:T(8,128)(2,1)} %all-gather.7.cloned.1.call-done, f32[5376]{0:T(1024)S(1)} %copy-done.4, f32[512]{0:T(512)S(1)} %add_rsqrt_fusion.2, bf16[512,10752]{0,1:T(8,128)(2,1)} %copy-done.1, s32[]{:T(128)S(6)} %select_n.18), kind=kOutput, calls=%fused_computation.52 | convolution fusion | flops 2830104576 | bytes 12090372 | tf_op jit(solution)/shard_map/dot_general | solution.py:36
  126.2 0.3 copy.19
  126.6 0.3 multiply_multiply_fusion.1
  126.9 0.4 subtract_convert_fusion
  127.4 0.3 pad_maximum_fusion
  127.7 4.4 %collective-permute-start.5 = (bf16[512,4,128]{2,0,1:T(8,128)(2,1)S(1)}, bf16[512,4,128]{2,0,1:T(8,128)(2,1)S(1)}, u32[]{:S(2)}, u32[]{:S(2)}) collective-permute-start(bf16[512,4,128]{2,0,1:T(8,128)(2,1)S(1)} %pad_maximum_fusion), channel_id=1, source_target_pairs={{0,16},{8,24},{16,32},{24,40},{32,48},{40,56},{48,64},{56,72},{64,... | collective-permute-start | bytes 1572872 | tf_op jit(solution)/shard_map/ppermute | solution.py:15
  132.1 2.4 collective-permute-start.6
  134.5 9.2 %convolution_convert_fusion.1 = bf16[512,512]{0,1:T(8,128)(2,1)} fusion(bf16[5376,512]{1,0:T(8,128)(2,1)} %all-gather.5.cloned.1.call-done, f32[5376]{0:T(1024)S(1)} %copy-done.4, f32[512]{0:T(512)S(1)} %add_rsqrt_fusion.2, bf16[512,10752]{0,1:T(8,128)(2,1)} %copy-done.1, s32[]{:T(128)S(6)} %select_n.18), kind=kOutput, calls=%fused_computation.47 | convolution fusion | flops 2829844480 | bytes 11557892 | tf_op jit(solution)/shard_map/dot_general | solution.py:36
  143.7 5.8 %collective-permute-start.3 = (bf16[512,4,128]{0,2,1:T(8,128)(2,1)}, bf16[512,4,128]{0,2,1:T(8,128)(2,1)}, u32[]{:S(2)}, u32[]{:S(2)}) collective-permute-start(bf16[512,4,128]{0,2,1:T(8,128)(2,1)} %bitcast), channel_id=1, source_target_pairs={{0,16},{8,24},{16,32},{24,40},{32,48},{40,56},{48,64},{56,72},{64,... | collective-permute-start | bytes 1572872 | tf_op jit(solution)/shard_map/ppermute | solution.py:15
  149.5 3.9 collective-permute-start.4
  153.5 5.2 %collective-permute-done.6 = bf16[512,4,128]{2,0,1:T(8,128)(2,1)S(1)} collective-permute-done((bf16[512,4,128]{2,0,1:T(8,128)(2,1)S(1)}, bf16[512,4,128]{2,0,1:T(8,128)(2,1)S(1)}, u32[]{:S(2)}, u32[]{:S(2)}) %collective-permute-start.6) | collective-permute-done | bytes 524320 | tf_op jit(solution)/shard_map/ppermute | solution.py:15
  158.7 1.5 maximum_bitcast_fusion.1
  160.2 13.5 %collective-permute-done.3 = bf16[512,4,128]{0,2,1:T(8,128)(2,1)} collective-permute-done((bf16[512,4,128]{0,2,1:T(8,128)(2,1)}, bf16[512,4,128]{0,2,1:T(8,128)(2,1)}, u32[]{:S(2)}, u32[]{:S(2)}) %collective-permute-start.3) | collective-permute-done | bytes 524320 | tf_op jit(solution)/shard_map/ppermute | solution.py:15
  173.7 11.2 %collective-permute-done.4 = bf16[512,4,128]{0,2,1:T(8,128)(2,1)} collective-permute-done((bf16[512,4,128]{0,2,1:T(8,128)(2,1)}, bf16[512,4,128]{0,2,1:T(8,128)(2,1)}, u32[]{:S(2)}, u32[]{:S(2)}) %collective-permute-start.4) | collective-permute-done | bytes 524320 | tf_op jit(solution)/shard_map/ppermute | solution.py:15
  184.9 2.6 maximum_bitcast_fusion
  187.5 48.0 %all-gather.9.cloned.1.call-done = bf16[5376,1024]{1,0:T(8,128)(2,1)} async-done(((bf16[336,1024]{1,0:T(8,128)(2,1)}), bf16[5376,1024]{1,0:T(8,128)(2,1)}) %all-gather.9.cloned.1.call-update) | async-done | bytes 11010064 | tf_op jit(solution)/shard_map/all_gather | solution.py:55
  235.5 11.8 %convolution_bitcast_fusion = f32[64,8,8,128]{3,1,2,0:T(8,128)S(1)} fusion(bf16[5376,1024]{1,0:T(8,128)(2,1)} %all-gather.9.cloned.1.call-done, f32[5376]{0:T(1024)S(1)} %copy-done.4, f32[512]{0:T(512)S(1)} %add_rsqrt_fusion.2, bf16[512,10752]{0,1:T(8,128)(2,1)} %copy-done.1, s32[]{:T(128)S(6)} %select_n.18), kind=kOutput, calls=%fused_computation.44 | convolution fusion | flops 5648154624 | bytes 18635780 | tf_op jit(solution)/shard_map/dot_general | solution.py:36
  247.3 0.5 copy.25
  247.8 0.6 multiply_reduce_fusion
  248.4 0.1 copy.20
  248.6 0.1 copy.21
  248.7 1.1 multiply_multiply_fusion
  249.8 1.1 multiply_subtract_fusion
  250.9 0.4 copy.22
  251.3 0.4 copy.23
  251.7 0.6 fusion.45
  252.3 46.3 %while.11 = (s32[]{:T(128)}, bf16[4,512,2,128]{1,3,2,0:T(8,128)(2,1)}, bf16[4,1536,128]{1,2,0:T(8,128)(2,1)}, bf16[4,1536,128]{2,1,0:T(8,128)(2,1)}, bf16[4,512,...) while((s32[]{:T(128)}, ...), condition=%wide.region_6.7_spmd.clone, body=%wide.region_3.6_spmd.clone.sunk | while | flops 817235456 | bytes 15486557 | solution.py:94
  252.4 1.2 fusion.74
  253.6 5.8 %fusion.75 = (f32[2,512]{1,0:T(2,128)S(1)}, f32[2,512,1536]{1,2,0:T(8,128)}) fusion(pred[512,1536]{0,1:T(8,128)(4,1)S(1)} %fusion.74, bf16[4,1536,128]{2,1,0:T(8,128)(2,1)} %get-tuple-element.159, s32[]{:T(128)} %get-tuple-element.147, bf16[4,512,2,128]{3,1,2,0:T(8,128)(2,1)S(1)} %get-tuple-element.160), kind=kOutput, calls=%fused_computation.73.clone.1 | convolution fusion | flops 407373312 | bytes 7738368 | tf_op jit(solution)/shard_map/while/body/eval_jaxpr/sub | solution.py:90
  259.4 4.3 %fusion.76 = bf16[4,512,2,128]{1,3,2,0:T(8,128)(2,1)} fusion(bf16[4,512,2,128]{1,3,2,0:T(8,128)(2,1)} %get-tuple-element.148, s32[]{:T(128)} %get-tuple-element.147, f32[2,512,1536]{1,2,0:T(8,128)} %get-tuple-element.136, f32[2,512]{1,0:T(2,128)S(1)} %get-tuple-element.137, bf16[4,1536,128]{1,2,0:T(8,128)(2,1)} %get-tuple-element.158), kind=kOutput, calls=%fused_computation.15.clone.1 | convolution fusion | flops 405929984 | bytes 6951936 | tf_op jit(solution)/shard_map/while/body/eval_jaxpr/grl,ld->rgd/dot_general | solution.py:91
  263.7 1.2 fusion.74
  264.9 5.8 %fusion.75 = (f32[2,512]{1,0:T(2,128)S(1)}, f32[2,512,1536]{1,2,0:T(8,128)}) fusion(pred[512,1536]{0,1:T(8,128)(4,1)S(1)} %fusion.74, bf16[4,1536,128]{2,1,0:T(8,128)(2,1)} %get-tuple-element.159, s32[]{:T(128)} %get-tuple-element.147, bf16[4,512,2,128]{3,1,2,0:T(8,128)(2,1)S(1)} %get-tuple-element.160), kind=kOutput, calls=%fused_computation.73.clone.1 | convolution fusion | flops 407373312 | bytes 7738368 | tf_op jit(solution)/shard_map/while/body/eval_jaxpr/sub | solution.py:90
  270.7 5.2 %fusion.76 = bf16[4,512,2,128]{1,3,2,0:T(8,128)(2,1)} fusion(bf16[4,512,2,128]{1,3,2,0:T(8,128)(2,1)} %get-tuple-element.148, s32[]{:T(128)} %get-tuple-element.147, f32[2,512,1536]{1,2,0:T(8,128)} %get-tuple-element.136, f32[2,512]{1,0:T(2,128)S(1)} %get-tuple-element.137, bf16[4,1536,128]{1,2,0:T(8,128)(2,1)} %get-tuple-element.158), kind=kOutput, calls=%fused_computation.15.clone.1 | convolution fusion | flops 405929984 | bytes 6951936 | tf_op jit(solution)/shard_map/while/body/eval_jaxpr/grl,ld->rgd/dot_general | solution.py:91
  275.8 1.2 fusion.74
  277.0 5.8 %fusion.75 = (f32[2,512]{1,0:T(2,128)S(1)}, f32[2,512,1536]{1,2,0:T(8,128)}) fusion(pred[512,1536]{0,1:T(8,128)(4,1)S(1)} %fusion.74, bf16[4,1536,128]{2,1,0:T(8,128)(2,1)} %get-tuple-element.159, s32[]{:T(128)} %get-tuple-element.147, bf16[4,512,2,128]{3,1,2,0:T(8,128)(2,1)S(1)} %get-tuple-element.160), kind=kOutput, calls=%fused_computation.73.clone.1 | convolution fusion | flops 407373312 | bytes 7738368 | tf_op jit(solution)/shard_map/while/body/eval_jaxpr/sub | solution.py:90
  282.9 4.4 %fusion.76 = bf16[4,512,2,128]{1,3,2,0:T(8,128)(2,1)} fusion(bf16[4,512,2,128]{1,3,2,0:T(8,128)(2,1)} %get-tuple-element.148, s32[]{:T(128)} %get-tuple-element.147, f32[2,512,1536]{1,2,0:T(8,128)} %get-tuple-element.136, f32[2,512]{1,0:T(2,128)S(1)} %get-tuple-element.137, bf16[4,1536,128]{1,2,0:T(8,128)(2,1)} %get-tuple-element.158), kind=kOutput, calls=%fused_computation.15.clone.1 | convolution fusion | flops 405929984 | bytes 6951936 | tf_op jit(solution)/shard_map/while/body/eval_jaxpr/grl,ld->rgd/dot_general | solution.py:91
  287.3 1.2 fusion.74
  288.5 5.8 %fusion.75 = (f32[2,512]{1,0:T(2,128)S(1)}, f32[2,512,1536]{1,2,0:T(8,128)}) fusion(pred[512,1536]{0,1:T(8,128)(4,1)S(1)} %fusion.74, bf16[4,1536,128]{2,1,0:T(8,128)(2,1)} %get-tuple-element.159, s32[]{:T(128)} %get-tuple-element.147, bf16[4,512,2,128]{3,1,2,0:T(8,128)(2,1)S(1)} %get-tuple-element.160), kind=kOutput, calls=%fused_computation.73.clone.1 | convolution fusion | flops 407373312 | bytes 7738368 | tf_op jit(solution)/shard_map/while/body/eval_jaxpr/sub | solution.py:90
  294.3 4.4 %fusion.76 = bf16[4,512,2,128]{1,3,2,0:T(8,128)(2,1)} fusion(bf16[4,512,2,128]{1,3,2,0:T(8,128)(2,1)} %get-tuple-element.148, s32[]{:T(128)} %get-tuple-element.147, f32[2,512,1536]{1,2,0:T(8,128)} %get-tuple-element.136, f32[2,512]{1,0:T(2,128)S(1)} %get-tuple-element.137, bf16[4,1536,128]{1,2,0:T(8,128)(2,1)} %get-tuple-element.158), kind=kOutput, calls=%fused_computation.15.clone.1 | convolution fusion | flops 405929984 | bytes 6951936 | tf_op jit(solution)/shard_map/while/body/eval_jaxpr/grl,ld->rgd/dot_general | solution.py:91
  298.6 20.8 %all-gather.11.cloned.1.call-done = bf16[1024,5376]{0,1:T(8,128)(2,1)} async-done(((bf16[1024,336]{0,1:T(8,128)(2,1)}), bf16[1024,5376]{0,1:T(8,128)(2,1)}) %all-gather.11.cloned.1.call-update) | async-done | bytes 11010064 | tf_op jit(solution)/shard_map/all_gather | solution.py:98
  319.5 10.4 %convolution_convert_fusion = bf16[512,5376]{0,1:T(8,128)(2,1)} fusion(bf16[1024,5376]{0,1:T(8,128)(2,1)} %all-gather.11.cloned.1.call-done, bf16[512,1024]{0,1:T(8,128)(2,1)} %bitcast.83), kind=kOutput, calls=%fused_computation.37 | convolution fusion | flops 5639897088 | bytes 17563648 | tf_op jit(solution)/shard_map/dot_general | solution.py:96
  329.9 57.3 %reduce-scatter.2.cloned.1.call-done = bf16[512,1344]{0,1:T(8,128)(2,1)} async-done(((bf16[512,5376]{0,1:T(8,128)(2,1)}), bf16[512,1344]{0,1:T(8,128)(2,1)}) %reduce-scatter.2.cloned.1.call-update) | async-done | bytes 1376272 | tf_op jit(solution)/shard_map/reduce_scatter | solution.py:101
  (26 shorter events, 0.2 us)
Async XLA Ops:
  6.5 101.9 %copy-start = (bf16[512,1344]{0,1:T(8,128)(2,1)S(1)}, bf16[512,1344]{0,1:T(8,128)(2,1)}, u32[]{:S(2)}) copy-start(bf16[512,1344]{0,1:T(8,128)(2,1)} %param.10) | copy-start | bytes 4128772
  6.5 111.1 %all-gather.7.cloned.1.call-start = ((), (), s32[]{:S(2)}) async-start(), calls=%async_computation.2 | async-start | bytes 5849088 | tf_op jit(solution)/shard_map/all_gather | solution.py:56
  7.3 127.3 %all-gather.5.cloned.1.call-start = ((), (), s32[]{:S(2)}) async-start(), calls=%async_computation.1 | async-start | bytes 5849088 | tf_op jit(solution)/shard_map/all_gather | solution.py:57
  8.0 227.5 %all-gather.9.cloned.1.call-start = ((), (), s32[]{:S(2)}) async-start(), calls=%async_computation.3 | async-start | bytes 11698176 | tf_op jit(solution)/shard_map/all_gather | solution.py:55
  8.7 310.7 %all-gather.11.cloned.1.call-start = ((), (), s32[]{:S(2)}) async-start(), calls=%async_computation.4 | async-start | bytes 11698176 | tf_op jit(solution)/shard_map/all_gather | solution.py:98
  9.3 377.9 %reduce-scatter.2.cloned.1.call-start = ((), (), s32[]{:S(2)}) async-start(), calls=%async_computation.5 | async-start | bytes 6881280 | tf_op jit(solution)/shard_map/reduce_scatter | solution.py:101
  9.4 33.6 %collective-permute-start = (bf16[512,1344]{0,1:T(8,128)(2,1)}, bf16[512,1344]{0,1:T(8,128)(2,1)S(1)}, u32[]{:S(2)}, u32[]{:S(2)}) collective-permute-start(bf16[512,1344]{0,1:T(8,128)(2,1)} %param.10), channel_id=1, source_target_pairs={{0,2},{2,4},{4,6},{6,0},{1,3},{3,5},{5,7},{7,1},{8,10},{10,12},{12... | collective-permute-start | bytes 4128776 | tf_op jit(solution)/shard_map/ppermute | solution.py:42
  43.0 31.6 %collective-permute-start.1 = (bf16[512,1344]{0,1:T(8,128)(2,1)S(1)}, bf16[512,1344]{0,1:T(8,128)(2,1)}, u32[]{:S(2)}, u32[]{:S(2)}) collective-permute-start(bf16[512,1344]{0,1:T(8,128)(2,1)S(1)} %collective-permute-done), channel_id=1, source_target_pairs={{0,2},{2,4},{4,6},{6,0},{1,3},{3,5},{5,7},{7,1},{8,10},{10,12},{12... | collective-permute-start | bytes 4128776 | tf_op jit(solution)/shard_map/ppermute | solution.py:42
  74.6 30.9 %collective-permute-start.2 = (bf16[512,1344]{0,1:T(8,128)(2,1)}, bf16[512,1344]{0,1:T(8,128)(2,1)}, u32[]{:S(2)}, u32[]{:S(2)}) collective-permute-start(bf16[512,1344]{0,1:T(8,128)(2,1)} %collective-permute-done.1), channel_id=1, source_target_pairs={{0,2},{2,4},{4,6},{6,0},{1,3},{3,5},{5,7},{7,1},{8,10},{10,12},{12... | collective-permute-start | bytes 4128776 | tf_op jit(solution)/shard_map/ppermute | solution.py:42
  111.5 6.1 %copy-start.4 = (f32[5376]{0:T(1024)S(1)}, f32[5376]{0:T(1024)}, u32[]{:S(2)}) copy-start(f32[5376]{0:T(1024)} %param.11) | copy-start | bytes 64516
  111.7 4.0 %copy-start.1 = (bf16[512,10752]{0,1:T(8,128)(2,1)}, bf16[512,10752]{0,1:T(8,128)(2,1)S(1)}, u32[]{:S(2)}) copy-start(bf16[512,10752]{0,1:T(8,128)(2,1)S(1)} %constant_dynamic-update-slice_fusion) | copy-start | bytes 33030148
  117.6 9.0 %copy-start.2 = (f32[128]{0:T(128)S(1)}, f32[128]{0:T(128)}, u32[]{:S(2)}) copy-start(f32[128]{0:T(128)} %param.16) | copy-start | bytes 1540
  127.7 25.8 %collective-permute-start.5 = (bf16[512,4,128]{2,0,1:T(8,128)(2,1)S(1)}, bf16[512,4,128]{2,0,1:T(8,128)(2,1)S(1)}, u32[]{:S(2)}, u32[]{:S(2)}) collective-permute-start(bf16[512,4,128]{2,0,1:T(8,128)(2,1)S(1)} %pad_maximum_fusion), channel_id=1, source_target_pairs={{0,16},{8,24},{16,32},{24,40},{32,48},{40,56},{48,64},{56,72},{64,... | collective-permute-start | bytes 1572872 | tf_op jit(solution)/shard_map/ppermute | solution.py:15
  132.1 26.6 %collective-permute-start.6 = (bf16[512,4,128]{2,0,1:T(8,128)(2,1)S(1)}, bf16[512,4,128]{2,0,1:T(8,128)(2,1)S(1)}, u32[]{:S(2)}, u32[]{:S(2)}) collective-permute-start(bf16[512,4,128]{2,0,1:T(8,128)(2,1)S(1)} %pad_maximum_fusion), channel_id=1, source_target_pairs={{0,8},{8,16},{16,24},{24,32},{32,40},{40,48},{48,56},{56,64},{64,7... | collective-permute-start | bytes 1572872 | tf_op jit(solution)/shard_map/ppermute | solution.py:15
  143.7 30.0 %collective-permute-start.3 = (bf16[512,4,128]{0,2,1:T(8,128)(2,1)}, bf16[512,4,128]{0,2,1:T(8,128)(2,1)}, u32[]{:S(2)}, u32[]{:S(2)}) collective-permute-start(bf16[512,4,128]{0,2,1:T(8,128)(2,1)} %bitcast), channel_id=1, source_target_pairs={{0,16},{8,24},{16,32},{24,40},{32,48},{40,56},{48,64},{56,72},{64,... | collective-permute-start | bytes 1572872 | tf_op jit(solution)/shard_map/ppermute | solution.py:15
  149.5 35.4 %collective-permute-start.4 = (bf16[512,4,128]{0,2,1:T(8,128)(2,1)}, bf16[512,4,128]{0,2,1:T(8,128)(2,1)}, u32[]{:S(2)}, u32[]{:S(2)}) collective-permute-start(bf16[512,4,128]{0,2,1:T(8,128)(2,1)} %bitcast), channel_id=1, source_target_pairs={{0,8},{8,16},{16,24},{24,32},{32,40},{40,48},{48,56},{56,64},{64,7... | collective-permute-start | bytes 1572872 | tf_op jit(solution)/shard_map/ppermute | solution.py:15
  247.3 1.4 copy-start.3
Sparse Core Ops, SparseCore 0:
  9.5 61.0 all-gather.6
  72.7 57.3 all-gather.4
  132.2 103.2 all-gather.8
  237.5 81.8 all-gather.10
  330.1 57.1 reduce-scatter.1
